TPU v7x, 256 devices: a whole 4x4x8 slice. The times are simulated.
256 devices in a mesh: req: 4 (over x), blk: 64 (over z, y, core).
Axes of the slice: x: 4, y: 4, z: 8, core: 2. Of those that a mesh axis runs over, the one named last changes fastest.
Arguments:
- tokens: bfloat16 [4, 8192, 2048], P('req', 'blk'), may hold values from -6 to 6
- block_ids: int32 [4, 128], P('req', 'blk'), may hold values from 0 to 127, as said below
- lengths: int32 [4], P('req'), may hold values from 4097 to 8192, as said below
- page_table: int32 [4, 2, 128], P('req'), may hold values from 0 to 255, as said below
- qkv_weight: bfloat16 [2048, 3072], P(('req', 'blk')), may hold values from -0.125 to 0.125
- q_gain: float32 [256], replicated
- k_gain: float32 [256], replicated
Outputs:
- attended: bfloat16 [4, 8192, 2048], P('req', 'blk')
- kv_cache: bfloat16 [4, 256, 64, 512], P('req', 'blk')
Inputs may be any that keep to these rules, and one draw needn't show every extreme that they name: `lengths`: one prompt has length exactly 8192. `block_ids`: the two entries of one device are b and 127 - b; over a prompt the first entries are a permutation of 0 to 63. `page_table`: each prompt's entries are a permutation of 0 to 255.
All inputs are finite; a program needn't handle non-finite values.
Results may differ from a plain program's by a relative error of at most 0.013.
The roundings to bfloat16 on the way count: a program that leaves them out, or rounds other values in their place, can miss the bound.
Values may be sent and summed in bfloat16 or wider, within the bound.
A program may use at most 128 MiB of HBM per device.

v0:
```python
import math

import jax
import jax.numpy as jnp
from jax import lax
from jax.sharding import PartitionSpec as P

H = 8
KVH = 2
HD = 256


ROPE_BASE = 1000000.0
NORM_EPS = 1e-06
FLOOR_SCORE = -1e30


def head_norm(tensor, scale_gain):
    return (
        tensor
        * lax.rsqrt(jnp.mean(tensor * tensor, axis=-1, keepdims=True) + NORM_EPS)
        * scale_gain
    )


def rotary(tensor, positions):
    half_dim = tensor.shape[-1] // 2
    channel = jnp.arange(half_dim).astype(jnp.float32)
    inverse = jnp.power(jnp.float32(ROPE_BASE), -2.0 * channel / tensor.shape[-1])
    angles = positions.astype(jnp.float32)[:, None] * inverse[None, :]
    cosine = jnp.cos(angles)[:, None, :]
    sine_part = jnp.sin(angles)[:, None, :]
    front_half = tensor[..., :half_dim]
    second = tensor[..., half_dim:]
    return jnp.concatenate(
        [front_half * cosine - second * sine_part, second * cosine + front_half * sine_part], -1
    )


def body(tokens, block_ids, lengths, page_table, qkv_weight, q_gain, k_gain):
    local_rows = tokens[0]
    row_count = local_rows.shape[0]
    blk_rows = row_count // 2
    groups = H // KVH
    projected = jnp.dot(
        local_rows,
        lax.all_gather(qkv_weight, ("req", "blk"), axis=0, tiled=True),
        preferred_element_type=jnp.float32,
    )
    own_ids = block_ids[0]
    positions = (
        own_ids[:, None] * blk_rows + jnp.arange(blk_rows, dtype=jnp.int32)[None, :]
    ).reshape(row_count)
    length = lengths[0]
    query_raw = projected[:, : H * HD].reshape(row_count, H, HD)
    key_raw = projected[:, H * HD : (H + KVH) * HD].reshape(row_count, KVH, HD)
    value_raw = projected[:, (H + KVH) * HD :].reshape(row_count, KVH, HD)
    queries = (
        rotary(head_norm(query_raw, q_gain), positions)
        .astype(jnp.bfloat16)
        .reshape(row_count, KVH, groups, HD)
    )
    send_keys = (
        rotary(head_norm(key_raw, k_gain), positions)
        .astype(jnp.bfloat16)
        .reshape(row_count, KVH * HD)
    )
    send_values = head_norm(value_raw, 1.0).astype(jnp.bfloat16).reshape(row_count, KVH * HD)
    all_ids = lax.all_gather(block_ids, "blk", axis=1, tiled=True)[0]
    table_size = all_ids.shape[0]
    slot_count = page_table.shape[1] * page_table.shape[2] // lax.axis_size("blk")
    my_slots = lax.axis_index("blk") * slot_count + jnp.arange(slot_count, dtype=jnp.int32)
    slot_match = page_table[0][None, :, :] == my_slots[:, None, None]
    head_grid = jnp.arange(page_table.shape[1], dtype=jnp.int32)[None, :, None]
    block_grid = jnp.arange(page_table.shape[2], dtype=jnp.int32)[None, None, :]
    slot_head = jnp.sum(jnp.where(slot_match, head_grid, 0), axis=(1, 2))
    slot_block = jnp.sum(jnp.where(slot_match, block_grid, 0), axis=(1, 2))
    query_live = positions < length
    running_max = jnp.full((row_count, KVH, groups), FLOOR_SCORE, jnp.float32)
    running_sum = jnp.zeros((row_count, KVH, groups), jnp.float32)
    weighted = jnp.zeros((row_count, KVH, groups, HD), jnp.float32)
    pages_out = jnp.zeros((slot_count, blk_rows, 2 * HD), jnp.bfloat16)
    piece_keys = lax.all_gather(send_keys, "blk", axis=0, tiled=True)
    piece_values = lax.all_gather(send_values, "blk", axis=0, tiled=True)
    piece_rows = piece_keys.shape[0]
    global_rows = jnp.arange(piece_rows, dtype=jnp.int32)
    block_index = global_rows // blk_rows
    lookup = jnp.sum(
        jnp.where(
            block_index[:, None] == jnp.arange(table_size, dtype=jnp.int32)[None, :],
            all_ids[None, :],
            0,
        ),
        1,
    )
    key_pos = lookup * blk_rows + global_rows % blk_rows
    key_heads = piece_keys.reshape(piece_rows, KVH, HD)
    value_heads = piece_values.reshape(piece_rows, KVH, HD)
    key_block = math.gcd(piece_rows, 512)

    def one_block(block_number, running):
        block_keys = lax.dynamic_slice_in_dim(key_heads, block_number * key_block, key_block, 0)
        block_values = lax.dynamic_slice_in_dim(value_heads, block_number * key_block, key_block, 0)
        block_pos = lax.dynamic_slice_in_dim(key_pos, block_number * key_block, key_block, 0)
        allowed = (block_pos[None, :] <= positions[:, None]) & (block_pos[None, :] < length)
        old_max, old_sum, old_weighted = running
        scores = jnp.einsum(
            "rgad,kgd->rgak", queries, block_keys, preferred_element_type=jnp.float32
        )
        mask_full = allowed[:, None, None, :]
        new_max = jnp.maximum(old_max, jnp.max(jnp.where(mask_full, scores, FLOOR_SCORE), -1))
        rescale = jnp.exp(old_max - new_max)
        weights = jnp.where(mask_full, jnp.exp(scores - new_max[..., None]), 0.0)
        new_sum = old_sum * rescale + jnp.sum(weights, -1)
        product = jnp.einsum(
            "rgak,kgd->rgad",
            weights.astype(jnp.bfloat16),
            block_values,
            preferred_element_type=jnp.float32,
        )
        return (new_max, new_sum, old_weighted * rescale[..., None] + product)

    running_max, running_sum, weighted = lax.fori_loop(
        0, piece_rows // key_block, one_block, (running_max, running_sum, weighted)
    )
    paired = jnp.concatenate([key_heads, value_heads], -1)
    row_numbers = jnp.arange(piece_rows, dtype=jnp.int32)
    page_offsets = jnp.arange(blk_rows, dtype=jnp.int32)
    page_list = []
    for slot_number in range(slot_count):
        target = slot_block[slot_number] * blk_rows
        is_start = key_pos == target
        present = jnp.any(is_start)
        first_row = jnp.sum(jnp.where(is_start, row_numbers, 0))
        rows_here = lax.dynamic_slice_in_dim(paired, first_row, blk_rows, 0)
        chosen = lax.dynamic_index_in_dim(rows_here, slot_head[slot_number], 1, keepdims=False)
        live_rows = target + page_offsets < length
        chosen = jnp.where(live_rows[:, None], chosen, jnp.zeros_like(chosen))
        page_list.append(jnp.where(present, chosen, pages_out[slot_number]))
    running_max, running_sum, weighted, pages_out = (
        running_max,
        running_sum,
        weighted,
        jnp.stack(page_list),
    )
    divisor = jnp.where(query_live[:, None, None], running_sum, 1.0)
    attended = jnp.where(query_live[:, None, None, None], weighted / divisor[..., None], 0.0)
    attended = attended.reshape(row_count, H * HD).astype(jnp.bfloat16)
    return (attended[None], pages_out[None])


def solution(mesh):
    in_specs = (
        P("req", "blk", None),
        P("req", "blk"),
        P("req"),
        P("req", None, None),
        P(("req", "blk"), None),
        P(),
        P(),
    )
    out_specs = (P("req", "blk", None), P("req", "blk", None, None))
    return jax.shard_map(body, mesh=mesh, in_specs=in_specs, out_specs=out_specs, check_vma=False)
```

profile of v0, /device:TPU:1, one launch (start us, length us, event | category | flops | bytes accessed | tf_op | source)
XLA Modules:
  0.0 402.0 jit_solution(17340536434207153513)
XLA Ops:
  8.0 128.9 %all-gather.4.cloned.1.call-done = bf16[2048,3072]{1,0:T(8,128)(2,1)} async-done(((bf16[8,3072]{1,0:T(8,128)(2,1)}), bf16[2048,3072]{1,0:T(8,128)(2,1)}) %all-gather.4.cloned.1.call-update) | async-done | bytes 12582928 | tf_op jit(solution)/shard_map/all_gather | solution.py:47
  136.8 6.4 %fusion.21 = f32[128,3072]{1,0:T(8,128)S(1)} fusion(bf16[2048,3072]{1,0:T(8,128)(2,1)} %all-gather.4.cloned.1.call-done, bf16[1,128,2048]{2,1,0:T(8,128)(2,1)S(1)} %copy-done), kind=kOutput, calls=%fused_computation.43 | convolution fusion | flops 1610612736 | bytes 14680064 | tf_op jit(solution)/shard_map/dot_general | solution.py:45
  146.1 0.8 copy.65
  157.0 16.9 %all-reduce = s32[128]{0:T(128)S(1)} all-reduce(s32[128]{0:T(128)S(1)} %bitcast_dynamic-update-slice_fusion), channel_id=1, replica_groups=mesh['req'=4,'blk'=64] {'blk'}, use_global_device_ids=true, to_apply=%add | all-reduce | flops 128 | bytes 1024
  173.9 2.5 select_reduce_fusion
  178.8 0.7 fusion.45
  192.6 32.3 %all-gather.8.cloned.1.call-done = bf16[8192,512]{1,0:T(8,128)(2,1)} async-done(((bf16[128,512]{1,0:T(8,128)(2,1)}), bf16[8192,512]{1,0:T(8,128)(2,1)}) %all-gather.8.cloned.1.call-update) | async-done | bytes 8388624 | tf_op jit(solution)/shard_map/all_gather | solution.py:84
  224.9 11.3 %copy.84 = bf16[8192,512]{0,1:T(8,128)(2,1)} copy(bf16[8192,512]{1,0:T(8,128)(2,1)} %all-gather.8.cloned.1.call-done) | data formatting | bytes 16777216
  236.2 74.7 %all-gather.6.cloned.1.call-done = bf16[8192,512]{0,1:T(8,128)(2,1)} async-done(((bf16[128,512]{0,1:T(8,128)(2,1)}), bf16[8192,512]{0,1:T(8,128)(2,1)}) %all-gather.6.cloned.1.call-update) | async-done | bytes 8388624 | tf_op jit(solution)/shard_map/all_gather | solution.py:83
  310.9 1.7 fusion.24
  313.0 77.7 %while.18 = (s32[]{:T(128)}, f32[128,2,4]{0,2,1:T(4,128)S(1)}, f32[128,2,4]{0,2,1:T(4,128)S(1)}, f32[128,2,4,256]{0,3,2,1:T(8,128)S(1)}, s32[8192]{0:T(1024)S(1)...) while((s32[]{:T(128)}, f32[128,2,4]{0,2,1:T(4,128)S(1)}, ...), condition=%wide.region_7.8_spmd.clone, body=%wide.region_4.0_spmd.clone.sunk | while | flops 541988480 | bytes 10298591 | solution.py:123
  313.2 0.7 broadcast_compare_fusion.10
  314.1 1.6 fusion.62
  316.1 1.7 fusion.65
  318.1 0.7 broadcast_compare_fusion.10
  319.0 1.6 fusion.62
  321.0 1.7 fusion.65
  323.9 1.6 fusion.62
  325.9 1.7 fusion.65
  328.7 1.6 fusion.62
  330.7 1.7 fusion.65
  333.6 1.6 fusion.62
  335.6 1.7 fusion.65
  338.4 1.6 fusion.62
  340.4 1.7 fusion.65
  343.3 1.6 fusion.62
  345.3 1.7 fusion.65
  348.2 1.6 fusion.62
  350.2 1.7 fusion.65
  353.0 1.6 fusion.62
  355.0 1.7 fusion.65
  357.9 1.6 fusion.62
  359.9 1.7 fusion.65
  362.7 1.6 fusion.62
  364.7 1.7 fusion.65
  367.6 1.6 fusion.62
  369.6 1.7 fusion.65
  372.4 1.6 fusion.62
  374.5 1.7 fusion.65
  377.3 1.6 fusion.62
  379.3 1.7 fusion.65
  382.2 1.6 fusion.62
  384.2 1.7 fusion.65
  387.0 1.6 fusion.62
  389.0 1.7 fusion.65
  390.9 1.0 copy.83
  393.9 0.8 fusion.27
  394.7 0.7 maximum_bitcast_fusion
  (203 shorter events, 34.8 us)
Async XLA Ops:
  7.2 129.7 %copy-start = (bf16[1,128,2048]{2,1,0:T(8,128)(2,1)S(1)}, bf16[1,128,2048]{2,1,0:T(8,128)(2,1)}, u32[]{:S(2)}) copy-start(bf16[1,128,2048]{2,1,0:T(8,128)(2,1)} %param.9) | copy-start | bytes 1572868
  7.2 129.6 %all-gather.4.cloned.1.call-start = ((), (), s32[]{:S(2)}) async-start(), calls=%async_computation | async-start | bytes 12632064 | tf_op jit(solution)/shard_map/all_gather | solution.py:47
  7.9 136.8 %copy-start.4 = (s32[1,2]{1,0:T(1,128)S(1)}, s32[1,2]{1,0:T(1,128)}, u32[]{:S(2)}) copy-start(s32[1,2]{1,0:T(1,128)} %param.10) | copy-start | bytes 28
  7.9 217.0 %all-gather.8.cloned.1.call-start = ((), (), s32[]{:S(2)}) async-start(), calls=%async_computation.2 | async-start | bytes 8519680 | tf_op jit(solution)/shard_map/all_gather | solution.py:84
  143.2 2.4 copy-start.1
  143.2 3.8 copy-start.3
  143.2 12.3 %copy-start.5 = (u32[256]{0:T(256)S(1)}, u32[256]{0:T(256)}, u32[]{:S(2)}) copy-start(u32[256]{0:T(256)} %constant.200) | copy-start | bytes 3076
  144.6 166.2 %all-gather.6.cloned.1.call-start = ((), (), s32[]{:S(2)}) async-start(), calls=%async_computation.1 | async-start | bytes 8519680 | tf_op jit(solution)/shard_map/all_gather | solution.py:83
  145.4 46.7 %copy-start.2 = (f32[256]{0:T(256)S(1)}, f32[256]{0:T(256)}, u32[]{:S(2)}) copy-start(f32[256]{0:T(256)} %param.14) | copy-start | bytes 3076
Sparse Core Ops, SparseCore 0:
  11.9 124.9 all-gather.3
  144.8 80.1 all-gather.7
  228.2 82.6 all-gather.5
where the time goes:
time: 404 us; the launch traced here: 402 us
  waiting for transfers between devices  237 us (59%)
  matrix products  59.4 us (15%)
  other arithmetic  37.3 us (9%)
  between operations  33 us (8%)
  local copies, waits for them, and re-layouts  17.7 us (4%)
  blocking collectives  16.9 us (4%)
    all_gather x1, waiting for transfers between devices, body(): lax.all_gather(qkv_weight, ('req', 'blk'), axis=0, tiled=True)  129 us
    all_gather x1, waiting for transfers between devices, body(): piece_keys = lax.all_gather(send_keys, 'blk', axis=0, tiled=True)  74.7 us
    all_gather x1, waiting for transfers between devices, body(): piece_values = lax.all_gather(send_values, 'blk', axis=0, tiled=True)  32.3 us
    dot_general x16, matrix products, one_block(): jnp.einsum('rgak,kgd->rgad', weights.astype(jnp.bfloat16), block_values,...  27.5 us
    dot_general x16, matrix products, one_block(): jnp.einsum('rgad,kgd->rgak', queries, block_keys, preferred_element_type=...  25.5 us
    unnamed x1, blocking collectives  16.9 us
    unnamed x18, local copies, waits for them, and re-layouts  12.4 us
    lt x16, other arithmetic, one_block(): block_pos[None, :] < length  11.6 us
  transfers between devices with their start and end apart: 3, of which 3 were waited for; matrix products, arithmetic and copies ran while one was open for 6% of the time, Pallas kernels for 0%

commit v1 on v0

v1 whole, which is shorter than its diff:
```python
import jax
import jax.numpy as jnp
from jax import lax
from jax.experimental import pallas as pl
from jax.experimental.pallas import tpu as pltpu
from jax.sharding import PartitionSpec as P

H = 8
KVH = 2
HD = 256
GRP = H // KVH
ROPE_BASE = 1000000.0
NORM_EPS = 1e-06
FLOOR_SCORE = -1e30
MESH = pl.DeviceIdType.MESH

NX, NY, NZ = 4, 4, 8
ROWS = 128
UNIT = 2 * ROWS + 16
CUTS = ((0, ROWS + 16), (ROWS + 16, ROWS))
STEPS = 16
T_FWD = 4
T_ATT = 9

OFFS = {"x": (1, 3, 2), "y": (1, 3, 2), "z": (1, 7, 2, 6, 3, 5, 4)}
SIZE = {"x": NX, "y": NY, "z": NZ}


def kernel(
    tok, meta, ids, w, qg, kg, tpos, length,
    out, pages,
    tokb, metab, idb, wtmp, wk, wv, wq, own, buf, qb, mb, lb, acc, pacc,
    osend, orecv, psend, precv,
    s_sib, r_sib, s_w, r_w, s_qx, r_qx, s_ring, r_ring, s_loc,
):
    r = lax.axis_index("req")
    b = lax.axis_index("blk")
    c = b % 2
    y = (b // 2) % NY
    z = b // (2 * NY)

    def dev(x_, y_, z_):
        return (x_, (z_ * NY + y_) * 2 + c)

    sib = (r, b + 1 - 2 * c)
    here = {"x": r, "y": y, "z": z}

    def along(ax, k):
        at = dict(here)
        at[ax] = (here[ax] + k) % SIZE[ax]
        return dev(at["x"], at["y"], at["z"])

    barrier = pltpu.get_barrier_semaphore()
    partners = [sib] + [along(ax, k) for ax in "xyz" for k in OFFS[ax]]
    for d in partners:
        pl.semaphore_signal(barrier, inc=1, device_id=d, device_id_type=MESH)
    pl.semaphore_wait(barrier, len(partners))

    def remote(src, dst, ss, rs, d):
        return pltpu.make_async_remote_copy(
            src_ref=src, dst_ref=dst, send_sem=ss, recv_sem=rs, device_id=d, device_id_type=MESH
        )

    mine = pl.ds(pl.multiple_of(c * ROWS, ROWS), ROWS)
    other = pl.ds(pl.multiple_of((1 - c) * ROWS, ROWS), ROWS)
    swap = [
        (w.at[1 - c], wtmp, wtmp),
        (tok, tokb.at[mine], tokb.at[other]),
        (meta, metab.at[mine], metab.at[other]),
        (ids, idb.at[c], idb.at[1 - c]),
    ]
    sends = []
    for i, (src, dst, _) in enumerate(swap):
        cp = remote(src, dst, s_sib.at[i], r_sib.at[i], sib)
        cp.start()
        sends.append(cp)

    def sib_recv(i):
        src, _, arrives = swap[i]
        remote(src, arrives, s_sib.at[i], r_sib.at[i], sib).wait_recv()

    local = [
        pltpu.make_async_copy(tok, tokb.at[mine], s_loc.at[0]),
        pltpu.make_async_copy(meta, metab.at[mine], s_loc.at[1]),
        pltpu.make_async_copy(ids, idb.at[c], s_loc.at[2]),
    ]
    for cp in local:
        cp.start()

    sib_recv(0)
    w_own = w[c].astype(jnp.float32)
    w_sib = wtmp[...].astype(jnp.float32)
    first = c == 0
    rows16 = jnp.concatenate(
        [jnp.where(first, w_own, w_sib), jnp.where(first, w_sib, w_own)], axis=0
    ).astype(jnp.bfloat16)
    wk[r, z, y] = rows16[:, :HD]
    wv[r, z, y] = rows16[:, HD : 2 * HD]
    wq[r, z, y] = rows16[:, 2 * HD :]

    def region(done, at):
        return tuple(slice(None) if ax in done else at[ax] for ax in "xzy")

    def phase(number, wb, done, ax):
        pairs = []
        for k, off in enumerate(OFFS[ax]):
            came = dict(here)
            came[ax] = (here[ax] - off + SIZE[ax]) % SIZE[ax]
            src = wb.at[region(done, here)]
            ss, rs, d = s_w.at[number, k], r_w.at[number, k], along(ax, off)
            pairs.append(
                (remote(src, src, ss, rs, d), remote(src, wb.at[region(done, came)], ss, rs, d))
            )
        for cp, _ in pairs:
            cp.start()
            sends.append(cp)
        return [arrive for _, arrive in pairs]

    def arrived(copies):
        for cp in copies:
            cp.wait_recv()

    k1 = phase(0, wk, "", "z")
    v1 = phase(1, wv, "", "z")
    q1 = phase(2, wq, "", "y")
    arrived(k1)
    k2 = phase(3, wk, "z", "y")
    arrived(v1)
    v2 = phase(4, wv, "z", "x")
    arrived(q1)
    q2 = phase(5, wq, "y", "z")
    arrived(k2)
    k3 = phase(6, wk, "zy", "x")
    arrived(v2)
    v3 = phase(7, wv, "zx", "y")

    mb[...] = jnp.full_like(mb, FLOOR_SCORE)
    lb[...] = jnp.zeros_like(lb)
    acc[...] = jnp.zeros_like(acc)
    pacc[...] = jnp.zeros_like(pacc)
    for i in (1, 2, 3):
        sib_recv(i)
    for cp in local:
        cp.wait()

    def normed(u, gain):
        scaled = u * lax.rsqrt(jnp.mean(u * u, axis=-1, keepdims=True) + NORM_EPS)
        return scaled if gain is None else scaled * gain[...]

    def rotated(u):
        half = HD // 2
        cosine = metab[:, :half]
        sine = metab[:, half : 2 * half]
        front, second = u[:, :half], u[:, half:]
        return jnp.concatenate(
            [front * cosine - second * sine, second * cosine + front * sine], axis=-1
        )

    def project(weights):
        return jnp.dot(
            tokb[...],
            weights.reshape(NX * NY * NZ * 16, HD),
            preferred_element_type=jnp.float32,
        )

    arrived(k3)
    keys = rotated(normed(project(wk[...]), kg)).astype(jnp.bfloat16)
    for i in range(2):
        own[i, :ROWS] = keys[i * ROWS : (i + 1) * ROWS]
        own[i, ROWS : ROWS + 16] = jnp.concatenate([idb[i], idb[i]], axis=-1)
    arrived(v3)
    values = normed(project(wv[...]), None).astype(jnp.bfloat16)
    for i in range(2):
        own[i, ROWS + 16 :] = values[i * ROWS : (i + 1) * ROWS]

    turn = y == (NY - 1 - z + NZ) % NY
    back = y == (NY - z + NZ) % NY

    def pick(cond, one, two):
        return tuple(jnp.where(cond, i, j) for i, j in zip(one, two))

    zp, zm, yp, ym = along("z", 1), along("z", NZ - 1), along("y", 1), along("y", NY - 1)
    to = [pick(turn, zp, yp), pick(back, zm, ym), pick(turn, yp, zp), pick(back, ym, zm)]

    def ring_copy(s, j, t, src):
        piece = pl.ds(*CUTS[j])
        return remote(
            src.at[piece], buf.at[s, t, piece], s_ring.at[s, t, j], r_ring.at[s, t, j], to[s]
        )

    for j in range(len(CUTS)):
        for s in range(4):
            ring_copy(s, j, 0, own.at[s // 2]).start()

    def ring_step(t):
        for j in range(len(CUTS)):
            for s in range(4):
                ring_copy(s, j, t, own.at[s // 2]).wait_recv()
                if s % 2 == 0:
                    ring_copy(s, j, t + 1, buf.at[s, t]).start()
                else:

                    @pl.when(t < STEPS - 2)
                    def _():
                        ring_copy(s, j, t + 1, buf.at[s, t]).start()

    def repeat(lo, hi, f):
        def go(t, carry):
            f(t)
            return carry

        lax.fori_loop(lo, hi, go, 0)

    halves = (pl.ds(0, NZ // 2), pl.ds(NZ // 2, NZ // 2))
    arrived(q2)
    nxt, prv = along("x", 1), along("x", NX - 1)
    x_prv, x_nxt, x_far = (r + NX - 1) % NX, (r + 1) % NX, (r + 2) % NX

    def q_copy(n, plane, half, d):
        ref = wq.at[plane, halves[half]]
        return remote(ref, ref, s_qx.at[n], r_qx.at[n], d)

    hop1 = [q_copy(0, r, 0, nxt), q_copy(1, r, 1, prv), q_copy(2, r, 1, nxt), q_copy(3, r, 0, prv)]
    for cp in hop1:
        cp.start()
        sends.append(cp)
    repeat(0, T_FWD, ring_step)
    arrived([q_copy(0, x_prv, 0, nxt), q_copy(1, x_nxt, 1, prv)])
    for cp in (q_copy(4, x_prv, 0, nxt), q_copy(5, x_nxt, 1, prv)):
        cp.start()
        sends.append(cp)
    repeat(T_FWD, T_ATT, ring_step)
    arrived(
        [
            q_copy(2, x_prv, 1, nxt),
            q_copy(3, x_nxt, 0, prv),
            q_copy(4, x_far, 0, nxt),
            q_copy(5, x_far, 1, prv),
        ]
    )

    def project_head(h):
        cols = pl.ds(pl.multiple_of(h * HD, HD), HD)
        rows = pl.ds(pl.multiple_of(h * 2 * ROWS, 2 * ROWS), 2 * ROWS)
        qb[rows, :] = rotated(normed(project(wq[:, :, :, :, cols]), qg)).astype(jnp.bfloat16)

    repeat(0, GRP, project_head)

    limit = length[0].astype(jnp.float32)
    lane = lax.broadcasted_iota(jnp.int32, (1, ROWS), 1)
    lane_in_block = (lane % (ROWS // 2)).astype(jnp.float32)

    def attend(units):
        key_pos = []
        for u in units:
            number = u[ROWS : ROWS + 16, :ROWS].astype(jnp.float32)[:1]
            key_pos.append(number * (ROWS // 2) + lane_in_block)
        seen = [jnp.where(kp < limit, kp, 1e9) for kp in key_pos]
        keys = jnp.concatenate([u[:ROWS] for u in units], axis=0)
        values = jnp.concatenate([u[ROWS + 16 :] for u in units], axis=0)

        def head(h):
            rows = pl.ds(pl.multiple_of(h * 2 * ROWS, 2 * ROWS), 2 * ROWS)
            query_pos = metab[:, HD : HD + ROWS]
            scores = lax.dot_general(
                qb[rows, :], keys, (((1,), (1,)), ((), ())), preferred_element_type=jnp.float32
            )
            parts = [
                jnp.where(sn <= query_pos, scores[:, i * ROWS : (i + 1) * ROWS], FLOOR_SCORE)
                for i, sn in enumerate(seen)
            ]
            old_max = mb[rows, :]
            top = parts[0]
            for part in parts[1:]:
                top = jnp.maximum(top, part)
            new_max = jnp.maximum(old_max, jnp.max(top, axis=-1, keepdims=True))
            rescale = jnp.exp(old_max - new_max)
            weights = [jnp.exp(part - new_max) for part in parts]
            total = weights[0]
            for wt in weights[1:]:
                total = total + wt
            mb[rows, :] = new_max
            lb[rows, :] = lb[rows, :] * rescale + total
            product = jnp.dot(
                jnp.concatenate([wt.astype(jnp.bfloat16) for wt in weights], axis=-1),
                values,
                preferred_element_type=jnp.float32,
            )
            acc[rows, :] = acc[rows, :] * jnp.concatenate([rescale, rescale], axis=-1) + product

        repeat(0, GRP, head)

        def page_part(i):
            rows = pl.ds(pl.multiple_of(i * 2 * ROWS, 2 * ROWS), 2 * ROWS)
            wanted = tpos[rows, :]
            chosen = jnp.concatenate(
                [jnp.where(wanted == kp, 1.0, 0.0).astype(jnp.bfloat16) for kp in key_pos], axis=-1
            )
            pacc[rows, :HD] += jnp.dot(chosen, keys, preferred_element_type=jnp.float32)
            pacc[rows, HD:] += jnp.dot(chosen, values, preferred_element_type=jnp.float32)

        repeat(0, 2, page_part)

    def attend_step(i):
        attend([buf[s, i] for s in range(4)])

    def both(t):
        ring_step(t)
        attend_step(2 * (t - T_ATT))
        attend_step(2 * (t - T_ATT) + 1)

    repeat(T_ATT, STEPS - 1, both)
    repeat(2 * (STEPS - 1 - T_ATT), STEPS - 1, attend_step)
    for j in range(len(CUTS)):
        for s in (0, 2):
            ring_copy(s, j, STEPS - 1, own.at[s // 2]).wait_recv()
    attend([own[0], own[1], buf[0, STEPS - 1], buf[2, STEPS - 1]])

    def result(part, h):
        start = h * 2 * ROWS + part * ROWS
        rows = pl.ds(pl.multiple_of(start, ROWS), ROWS)
        live = metab[pl.ds(pl.multiple_of(part * ROWS, ROWS), ROWS), HD : HD + 1] < limit
        total = jnp.sum(lb[rows, :], axis=-1, keepdims=True)
        divided = acc[rows, :] / jnp.where(live, total, 1.0)
        return jnp.where(live, divided, 0.0).astype(jnp.bfloat16)

    for h in range(GRP):
        osend[:, h * HD : (h + 1) * HD] = result(1 - c, h)
    o_cp = remote(osend, orecv, s_sib.at[4], r_sib.at[4], sib)
    o_cp.start()
    half = 4 * 64
    theirs = pl.ds(pl.multiple_of((1 - c) * half, half), half)
    psend[...] = pacc[theirs, :].astype(jnp.bfloat16)
    p_cp = remote(psend, precv, s_sib.at[5], r_sib.at[5], sib)
    p_cp.start()
    my_cols = pl.multiple_of(c * GRP * HD, GRP * HD)
    for h in range(GRP):
        out[:, pl.ds(my_cols + h * HD, HD)] = result(c, h)
    p_cp.wait()
    ours = pl.ds(pl.multiple_of(c * half, half), half)
    pages[...] = (pacc[ours, :] + precv[...].astype(jnp.float32)).astype(jnp.bfloat16)
    o_cp.wait()
    out[:, pl.ds(pl.multiple_of((1 - c) * GRP * HD, GRP * HD), GRP * HD)] = orecv[...]

    for cp in sends:
        cp.wait_send()

    def ring_sent(t):
        for j in range(len(CUTS)):
            for s in range(4):
                if s % 2 == 0:
                    ring_copy(s, j, t, own.at[s // 2]).wait_send()
                else:

                    @pl.when(t < STEPS - 1)
                    def _():
                        ring_copy(s, j, t, own.at[s // 2]).wait_send()

    repeat(0, STEPS, ring_sent)


def body(tokens, block_ids, lengths, page_table, qkv_weight, q_gain, k_gain):
    own_ids = block_ids[0]
    blk_rows = ROWS // 2
    positions = (
        own_ids[:, None] * blk_rows + jnp.arange(blk_rows, dtype=jnp.int32)[None, :]
    ).reshape(ROWS)
    half = HD // 2
    channel = jnp.arange(half).astype(jnp.float32)
    inverse = jnp.power(jnp.float32(ROPE_BASE), -2.0 * channel / HD)
    pos_f = positions.astype(jnp.float32)
    angles = pos_f[:, None] * inverse[None, :]
    meta = jnp.concatenate(
        [jnp.cos(angles), jnp.sin(angles), jnp.broadcast_to(pos_f[:, None], (ROWS, ROWS))], axis=-1
    )
    ids = jnp.broadcast_to(
        jnp.repeat(own_ids, blk_rows).astype(jnp.bfloat16)[None, :], (16, ROWS)
    )
    blk = lax.axis_index("blk")
    core = blk % 2
    w = jnp.stack(
        [
            jnp.concatenate(
                [
                    qkv_weight[:, H * HD + g * HD : H * HD + (g + 1) * HD],
                    qkv_weight[:, (H + KVH + g) * HD : (H + KVH + g + 1) * HD],
                    qkv_weight[:, g * GRP * HD : (g + 1) * GRP * HD],
                ],
                axis=-1,
            )
            for g in range(KVH)
        ]
    )
    my_slots = (blk // 2) * 8 + jnp.arange(8, dtype=jnp.int32)
    table = lax.dynamic_index_in_dim(page_table[0], core, 0, keepdims=False)
    match = table[None, :] == my_slots[:, None]
    block_no = jnp.sum(
        jnp.where(match, jnp.arange(table.shape[0], dtype=jnp.int32)[None, :] + 1, 0), axis=1
    ) - 1
    wanted = block_no[:, None] * blk_rows + jnp.arange(blk_rows, dtype=jnp.int32)[None, :]
    wanted = jnp.where((block_no[:, None] >= 0) & (wanted < lengths[0]), wanted, -1)
    tpos = jnp.broadcast_to(
        wanted.reshape(8 * blk_rows, 1).astype(jnp.float32), (8 * blk_rows, ROWS)
    )

    vm = pl.BlockSpec(memory_space=pltpu.VMEM)
    dma = pltpu.SemaphoreType.DMA
    bf, f32 = jnp.bfloat16, jnp.float32
    attended, cache = pl.pallas_call(
        kernel,
        out_shape=(
            jax.ShapeDtypeStruct((ROWS, H * HD), bf),
            jax.ShapeDtypeStruct((4 * 64, 2 * HD), bf),
        ),
        in_specs=[vm] * 7 + [pl.BlockSpec(memory_space=pltpu.SMEM)],
        out_specs=(vm, vm),
        scratch_shapes=[
            pltpu.VMEM((2 * ROWS, 2048), bf),
            pltpu.VMEM((2 * ROWS, 3 * ROWS), f32),
            pltpu.VMEM((2, 16, ROWS), bf),
            pltpu.VMEM((8, 6 * HD), bf),
            pltpu.VMEM((NX, NZ, NY, 16, HD), bf),
            pltpu.VMEM((NX, NZ, NY, 16, HD), bf),
            pltpu.VMEM((NX, NZ, NY, 16, GRP * HD), bf),
            pltpu.VMEM((2, UNIT, HD), bf),
            pltpu.VMEM((4, STEPS, UNIT, HD), bf),
            pltpu.VMEM((GRP * 2 * ROWS, HD), bf),
            pltpu.VMEM((GRP * 2 * ROWS, ROWS), f32),
            pltpu.VMEM((GRP * 2 * ROWS, ROWS), f32),
            pltpu.VMEM((GRP * 2 * ROWS, HD), f32),
            pltpu.VMEM((8 * 64, 2 * HD), f32),
            pltpu.VMEM((ROWS, GRP * HD), bf),
            pltpu.VMEM((ROWS, GRP * HD), bf),
            pltpu.VMEM((4 * 64, 2 * HD), bf),
            pltpu.VMEM((4 * 64, 2 * HD), bf),
            dma((6,)),
            dma((6,)),
            dma((8, 7)),
            dma((8, 7)),
            dma((6,)),
            dma((6,)),
            dma((4, STEPS, len(CUTS))),
            dma((4, STEPS, len(CUTS))),
            dma((3,)),
        ],
        compiler_params=pltpu.CompilerParams(
            collective_id=0, has_side_effects=True, vmem_limit_bytes=56 << 20
        ),
        name="prefill",
    )(
        tokens[0],
        meta,
        ids,
        w,
        q_gain.reshape(1, HD),
        k_gain.reshape(1, HD),
        tpos,
        lengths,
    )
    return (attended[None], cache.reshape(1, 4, 64, 2 * HD))


def solution(mesh):
    in_specs = (
        P("req", "blk", None),
        P("req", "blk"),
        P("req"),
        P("req", None, None),
        P(("req", "blk"), None),
        P(),
        P(),
    )
    out_specs = (P("req", "blk", None), P("req", "blk", None, None))
    return jax.shard_map(body, mesh=mesh, in_specs=in_specs, out_specs=out_specs, check_vma=False)
```

time: 404 us -> 148 us (0.37)
  waiting for transfers between devices: 237 us -> 0 us
  Pallas kernels: 0 us -> 140 us
  matrix products: 59.4 us -> 0 us
  other arithmetic: 37.3 us -> 2 us
  between operations: 33 us -> 1.41 us
  blocking collectives: 16.9 us -> 0 us
  local copies, waits for them, and re-layouts: 17.7 us -> 5.21 us
    all_gather x3 -> x0, waiting for transfers between devices: 236 us -> none  [the longest x1 129 us: body(): lax.all_gather(qkv_weight, ('req', 'blk'), axis=0, tiled=True)]
    pallas_call x0 -> x1, Pallas kernels: none -> 140 us  [body(): pl.pallas_call(kernel, out_shape=(jax.ShapeDtypeStruct((ROWS, H * HD), bf...]
    dot_general x33 -> x0, matrix products: 59.4 us -> none  [the longest x16 27.5 us: one_block(): jnp.einsum('rgak,kgd->rgad', weights.astype(jnp.bfloat16), block_values,...]
    unnamed x1 -> x0, blocking collectives: 16.9 us -> none
    reduce_sum x25 -> x1, other arithmetic: 12 us -> 0.18 us  [body(): jnp.sum(jnp.where(match, jnp.arange(table.shape[0], dtype=jnp.int32)[None...]
    lt x21 -> x0, other arithmetic: 11.7 us -> none  [the longest x16 11.6 us: one_block(): block_pos[None, :] < length]
    unnamed x18 -> x10, local copies, waits for them, and re-layouts: 12.4 us -> 3.22 us
  transfers between devices with their start and end apart: 3 -> 0, of which waited for: 3 -> 0; matrix products, arithmetic and copies ran while one was open for 6% -> 0% of each run, Pallas kernels for 0% -> 0%
where the time goes in v1:
time: 148 us
  Pallas kernels  140 us (95%)
  local copies, waits for them, and re-layouts  5.21 us (4%)
  other arithmetic  2 us (1%)
    pallas_call x1, Pallas kernels, body(): pl.pallas_call(kernel, out_shape=(jax.ShapeDtypeStruct((ROWS, H * HD), bf...  140 us
    unnamed x10, local copies, waits for them, and re-layouts  3.22 us

profile of v1, /device:TPU:1, one launch (start us, length us, event | category | flops | bytes accessed | tf_op | source)
XLA Modules:
  0.0 148.2 jit_solution(17587077146612803900)
XLA Ops:
  0.6 0.0 copy-start
  0.7 0.0 copy-start.2
  1.3 0.0 copy-done
  1.4 0.2 select_reduce_fusion
  1.6 0.1 and.28
  1.7 0.0 copy-start.3
  1.7 0.1 and.29
  1.8 0.6 copy-done.3
  2.3 0.1 broadcast_in_dim.23
  2.4 0.1 convert_element_type.44
  2.5 0.1 add_convert_fusion
  2.6 0.1 convert_element_type.40
  2.6 0.6 broadcast_in_dim.24.ids
  3.2 0.1 iota_add_fusion
  3.3 0.1 add.90
  3.4 0.0 copy-done.2
  3.4 0.6 pad_maximum_fusion.1.w
  4.1 0.1 mul.40
  4.1 0.3 multiply_cosine_fusion
  4.4 0.7 pad_maximum_fusion.meta
  5.1 0.8 broadcast_in_dim.29.tpos
  6.0 139.5 %prefill.1 = (bf16[128,2048]{1,0:T(8,128)(2,1)}, bf16[256,512]{1,0:T(8,128)(2,1)}) custom-call(bf16[128,2048]{1,0:T(8,128)(2,1)} %bitcast.17, f32[128,384]{1,0:T(8,128)} %pad_maximum_fusion.meta, bf16[16,128]{1,0:T(8,128)(2,1)} %broadcast_in_dim.24.ids, bf16[2,8,1536]{2,1,0:T(8,128)(2,1)} %pad_maximum_fusion.1.w, f32[1,256]{1,0:T(1,128)} %bitcast.20, ...), custom_call_target="tpu_custom_call" | custom-call | tf_op jit(solution)/shard_map/prefill/pallas_call | solution.py:409
  145.5 0.0 copy-start.1
  145.5 1.9 %copy.12 = bf16[1,128,2048]{2,1,0:T(8,128)(2,1)} copy(bf16[1,128,2048]{2,1,0:T(8,128)(2,1)} %bitcast.18) | data formatting | bytes 1048576
  147.5 0.0 copy-done.1
  147.5 0.7 copy.13
  (11 shorter events, 0.1 us)
Async XLA Ops:
  0.6 0.7 copy-start
  0.7 2.7 %copy-start.2 = (bf16[8,3072]{1,0:T(8,128)(2,1)S(1)}, bf16[8,3072]{1,0:T(8,128)(2,1)}, u32[]{:S(2)}) copy-start(bf16[8,3072]{1,0:T(8,128)(2,1)} %param.11) | copy-start | bytes 147460
  1.7 0.7 copy-start.3
  145.5 1.9 %copy-start.1 = (bf16[256,512]{1,0:T(8,128)(2,1)S(1)}, bf16[256,512]{1,0:T(8,128)(2,1)}, u32[]{:S(2)}) copy-start(bf16[256,512]{1,0:T(8,128)(2,1)} %get-tuple-element.5) | copy-start | bytes 786436

commit v2 on v1

--- a/solution.py
+++ b/solution.py
@@ -260,7 +260,7 @@
         values = jnp.concatenate([u[ROWS + 16 :] for u in units], axis=0)
 
         def head(h):
-            rows = pl.ds(pl.multiple_of(h * 2 * ROWS, 2 * ROWS), 2 * ROWS)
+            rows = pl.ds(h * 2 * ROWS, 2 * ROWS)
             query_pos = metab[:, HD : HD + ROWS]
             scores = lax.dot_general(
                 qb[rows, :], keys, (((1,), (1,)), ((), ())), preferred_element_type=jnp.float32
@@ -288,7 +288,8 @@
             )
             acc[rows, :] = acc[rows, :] * jnp.concatenate([rescale, rescale], axis=-1) + product
 
-        repeat(0, GRP, head)
+        for h in range(GRP):
+            head(h)
 
         def page_part(i):
             rows = pl.ds(pl.multiple_of(i * 2 * ROWS, 2 * ROWS), 2 * ROWS)
@@ -299,7 +300,8 @@
             pacc[rows, :HD] += jnp.dot(chosen, keys, preferred_element_type=jnp.float32)
             pacc[rows, HD:] += jnp.dot(chosen, values, preferred_element_type=jnp.float32)
 
-        repeat(0, 2, page_part)
+        for i in range(2):
+            page_part(i)
 
     def attend_step(i):
         attend([buf[s, i] for s in range(4)])

time: 148 us -> 130 us (0.88)
  Pallas kernels: 140 us -> 121 us
    pallas_call x1, Pallas kernels: 140 us -> 121 us  [body(): pl.pallas_call(kernel, out_shape=(jax.ShapeDtypeStruct((ROWS, H * HD), bf...]
where the time goes in v2:
time: 130 us
  Pallas kernels  121 us (93%)
  local copies, waits for them, and re-layouts  5.21 us (4%)
  other arithmetic  2 us (2%)
  between operations  1.41 us (1%)
    pallas_call x1, Pallas kernels, body(): pl.pallas_call(kernel, out_shape=(jax.ShapeDtypeStruct((ROWS, H * HD), bf...  121 us
    unnamed x10, local copies, waits for them, and re-layouts  3.22 us

profile of v2, /device:TPU:1, one launch (start us, length us, event | category | flops | bytes accessed | tf_op | source)
XLA Modules:
  0.0 129.5 jit_solution(4813706420793032582)
XLA Ops:
  0.6 0.0 copy-start
  0.7 0.0 copy-start.2
  1.3 0.0 copy-done
  1.4 0.2 select_reduce_fusion
  1.6 0.1 and.28
  1.7 0.0 copy-start.3
  1.7 0.1 and.29
  1.8 0.6 copy-done.3
  2.3 0.1 broadcast_in_dim.23
  2.4 0.1 convert_element_type.44
  2.5 0.1 add_convert_fusion
  2.6 0.1 convert_element_type.40
  2.6 0.6 broadcast_in_dim.24.ids
  3.2 0.1 iota_add_fusion
  3.3 0.1 add.90
  3.4 0.0 copy-done.2
  3.4 0.6 pad_maximum_fusion.1.w
  4.1 0.1 mul.40
  4.1 0.3 multiply_cosine_fusion
  4.4 0.7 pad_maximum_fusion.meta
  5.1 0.8 broadcast_in_dim.29.tpos
  6.0 120.9 %prefill.1 = (bf16[128,2048]{1,0:T(8,128)(2,1)}, bf16[256,512]{1,0:T(8,128)(2,1)}) custom-call(bf16[128,2048]{1,0:T(8,128)(2,1)} %bitcast.17, f32[128,384]{1,0:T(8,128)} %pad_maximum_fusion.meta, bf16[16,128]{1,0:T(8,128)(2,1)} %broadcast_in_dim.24.ids, bf16[2,8,1536]{2,1,0:T(8,128)(2,1)} %pad_maximum_fusion.1.w, f32[1,256]{1,0:T(1,128)} %bitcast.20, ...), custom_call_target="tpu_custom_call" | custom-call | tf_op jit(solution)/shard_map/prefill/pallas_call | solution.py:411
  126.9 0.0 copy-start.1
  126.9 1.9 %copy.12 = bf16[1,128,2048]{2,1,0:T(8,128)(2,1)} copy(bf16[1,128,2048]{2,1,0:T(8,128)(2,1)} %bitcast.18) | data formatting | bytes 1048576
  128.8 0.0 copy-done.1
  128.8 0.7 copy.13
  (11 shorter events, 0.1 us)
Async XLA Ops:
  0.6 0.7 copy-start
  0.7 2.7 %copy-start.2 = (bf16[8,3072]{1,0:T(8,128)(2,1)S(1)}, bf16[8,3072]{1,0:T(8,128)(2,1)}, u32[]{:S(2)}) copy-start(bf16[8,3072]{1,0:T(8,128)(2,1)} %param.11) | copy-start | bytes 147460
  1.7 0.7 copy-start.3
  126.9 1.9 %copy-start.1 = (bf16[256,512]{1,0:T(8,128)(2,1)S(1)}, bf16[256,512]{1,0:T(8,128)(2,1)}, u32[]{:S(2)}) copy-start(bf16[256,512]{1,0:T(8,128)(2,1)} %get-tuple-element.5) | copy-start | bytes 786436

commit v3 on v2

v3 whole, which is shorter than its diff:
```python
import jax
import jax.numpy as jnp
from jax import lax
from jax.experimental import pallas as pl
from jax.experimental.pallas import tpu as pltpu
from jax.sharding import PartitionSpec as P

H = 8
KVH = 2
HD = 256
GRP = H // KVH
ROPE_BASE = 1000000.0
NORM_EPS = 1e-06
FLOOR_SCORE = -1e30
MESH = pl.DeviceIdType.MESH

NX, NY, NZ = 4, 4, 8
ROWS = 128
UNIT = 2 * ROWS + 16
PIECES = ((0, ROWS + 16), (ROWS + 16, ROWS))
ORDER = ["a0", "b0", "a1", "a7", "b1", "b7", "a2", "a6", "b2", "b6", "a3", "a5", "b3", "b5", "a4", "b4"]
SLOT = {name: i for i, name in enumerate(ORDER)}

OFFS = {"x": (1, 3, 2), "y": (1, 3, 2), "z": (1, 7, 2, 6, 3, 5, 4)}
SIZE = {"x": NX, "y": NY, "z": NZ}


def kernel(
    tok, w, qg, kg, inverse, table, ids, length,
    out, pages,
    tokb, metab, idb, tpos, wout, wtmp, wk, wv, wq0, wq1, kv, qb, mb, lb, acc, pacc,
    osend, orecv, psend, precv,
    s_sib, r_sib, s_w, r_w, s_qx, r_qx, s_a, r_a, s_b, r_b, s_y, r_y, s_loc,
):
    r = lax.axis_index("req")
    b = lax.axis_index("blk")
    c = b % 2
    y = (b // 2) % NY
    z = b // (2 * NY)

    def dev(x_, y_, z_):
        return (x_, (z_ * NY + y_) * 2 + c)

    sib = (r, b + 1 - 2 * c)
    here = {"x": r, "y": y, "z": z}

    def along(ax, k):
        at = dict(here)
        at[ax] = (here[ax] + k) % SIZE[ax]
        return dev(at["x"], at["y"], at["z"])

    barrier = pltpu.get_barrier_semaphore()
    partners = [sib] + [along(ax, k) for ax in "xyz" for k in OFFS[ax]]
    for d in partners:
        pl.semaphore_signal(barrier, inc=1, device_id=d, device_id_type=MESH)
    pl.semaphore_wait(barrier, len(partners))

    def remote(src, dst, ss, rs, d):
        return pltpu.make_async_remote_copy(
            src_ref=src, dst_ref=dst, send_sem=ss, recv_sem=rs, device_id=d, device_id_type=MESH
        )

    mine = pl.ds(pl.multiple_of(c * ROWS, ROWS), ROWS)
    other = pl.ds(pl.multiple_of((1 - c) * ROWS, ROWS), ROWS)
    q_cols = GRP * HD

    def columns(core):
        at = lambda start, size: w[:, pl.ds(pl.multiple_of(start, HD), size)]
        return jnp.concatenate(
            [
                at((H + core) * HD, HD),
                at((H + KVH + core) * HD, HD),
                at(core * q_cols, q_cols),
            ],
            axis=-1,
        )

    wout[...] = columns(1 - c)
    swap = [
        (wout, wtmp, wtmp),
        (tok, tokb.at[mine], tokb.at[other]),
        (metab.at[mine], metab.at[mine], metab.at[other]),
        (idb.at[c], idb.at[c], idb.at[1 - c]),
    ]
    sends = []

    def sib_send(i):
        src, dst, _ = swap[i]
        cp = remote(src, dst, s_sib.at[i], r_sib.at[i], sib)
        cp.start()
        sends.append(cp)

    def sib_recv(i):
        src, _, arrives = swap[i]
        remote(src, arrives, s_sib.at[i], r_sib.at[i], sib).wait_recv()

    sib_send(0)
    sib_send(1)
    local = [pltpu.make_async_copy(tok, tokb.at[mine], s_loc.at[0])]
    for cp in local:
        cp.start()

    sib_recv(0)
    w_own = columns(c).astype(jnp.float32)
    w_sib = wtmp[...].astype(jnp.float32)
    first = c == 0
    rows16 = jnp.concatenate(
        [jnp.where(first, w_own, w_sib), jnp.where(first, w_sib, w_own)], axis=0
    ).astype(jnp.bfloat16)
    wk[r, z, y] = rows16[:, :HD]
    wv[r, z, y] = rows16[:, HD : 2 * HD]
    wq0[r, z, y] = rows16[:, 2 * HD : 4 * HD]
    wq1[r, z, y] = rows16[:, 4 * HD :]

    def region(done, at):
        return tuple(slice(None) if ax in done else at[ax] for ax in "xzy")

    def phase(number, wb, done, ax):
        pairs = []
        for k, off in enumerate(OFFS[ax]):
            came = dict(here)
            came[ax] = (here[ax] - off + SIZE[ax]) % SIZE[ax]
            src = wb.at[region(done, here)]
            ss, rs, d = s_w.at[number, k], r_w.at[number, k], along(ax, off)
            pairs.append(
                (remote(src, src, ss, rs, d), remote(src, wb.at[region(done, came)], ss, rs, d))
            )
        for cp, _ in pairs:
            cp.start()
            sends.append(cp)
        return [arrive for _, arrive in pairs]

    def arrived(copies):
        for cp in copies:
            cp.wait_recv()

    k1 = phase(0, wk, "", "z")
    v1 = phase(1, wv, "", "z")
    q01 = phase(2, wq0, "", "y")
    q11 = phase(3, wq1, "", "y")
    arrived(k1)
    k2 = phase(4, wk, "z", "y")
    arrived(v1)
    v2 = phase(5, wv, "z", "x")
    arrived(q01)
    q02 = phase(6, wq0, "y", "z")
    arrived(k2)
    k3 = phase(7, wk, "zy", "x")
    arrived(v2)
    v3 = phase(8, wv, "zx", "y")
    arrived(q11)
    q12 = phase(9, wq1, "y", "z")

    blk_rows = ROWS // 2
    row = lax.broadcasted_iota(jnp.int32, (ROWS, ROWS), 0)
    lane_no = lax.broadcasted_iota(jnp.int32, (16, ROWS), 1)
    pos = jnp.where(row < blk_rows, ids[0], ids[1]) * blk_rows + row % blk_rows
    pos_f = pos.astype(jnp.float32)
    angles = pos_f * inverse[...]
    metab[mine, :ROWS] = jnp.cos(angles)
    metab[mine, ROWS : 2 * ROWS] = jnp.sin(angles)
    metab[mine, 2 * ROWS :] = pos_f
    numbers = jnp.where(lane_no < blk_rows, ids[0], ids[1])
    idb[c] = numbers.astype(jnp.float32).astype(jnp.bfloat16)
    sib_send(2)
    sib_send(3)

    entries = table[pl.ds(c, 1), :]
    block_of = lax.broadcasted_iota(jnp.int32, (1, ROWS), 1).astype(jnp.float32)
    row_f = lax.broadcasted_iota(jnp.int32, (blk_rows, ROWS), 0).astype(jnp.float32)
    for i in range(8):
        slot = (b // 2) * 8 + i
        found = jnp.max(jnp.where(entries == slot, block_of, -1.0), axis=-1, keepdims=True)
        wanted = found * blk_rows + row_f
        keep = (found >= 0.0) & (wanted < length[0].astype(jnp.float32))
        tpos[i * blk_rows : (i + 1) * blk_rows, :] = jnp.where(keep, wanted, -1.0)

    mb[...] = jnp.full_like(mb, FLOOR_SCORE)
    lb[...] = jnp.zeros_like(lb)
    acc[...] = jnp.zeros_like(acc)
    pacc[...] = jnp.zeros_like(pacc)
    for i in (1, 2, 3):
        sib_recv(i)
    for cp in local:
        cp.wait()

    def normed(u, gain):
        scaled = u * lax.rsqrt(jnp.mean(u * u, axis=-1, keepdims=True) + NORM_EPS)
        return scaled if gain is None else scaled * gain[...]

    def rotated(u):
        half = HD // 2
        cosine = metab[:, :half]
        sine = metab[:, half : 2 * half]
        front, second = u[:, :half], u[:, half:]
        return jnp.concatenate(
            [front * cosine - second * sine, second * cosine + front * sine], axis=-1
        )

    def project(weights):
        return jnp.dot(
            tokb[...],
            weights.reshape(NX * NY * NZ * 16, HD),
            preferred_element_type=jnp.float32,
        )

    halves = (pl.ds(0, NZ // 2), pl.ds(NZ // 2, NZ // 2))
    nxt, prv = along("x", 1), along("x", NX - 1)
    x_prv, x_nxt, x_far = (r + NX - 1) % NX, (r + 1) % NX, (r + 2) % NX

    def q_copy(part, n, plane, half, d):
        ref = (wq0, wq1)[part].at[plane, halves[half]]
        return remote(ref, ref, s_qx.at[part, n], r_qx.at[part, n], d)

    def begin(copies):
        for cp in copies:
            cp.start()
            sends.append(cp)

    def q_hop1(p):
        begin(
            [
                q_copy(p, 0, r, 0, nxt),
                q_copy(p, 1, r, 1, prv),
                q_copy(p, 2, r, 1, nxt),
                q_copy(p, 3, r, 0, prv),
            ]
        )

    def q_hop2(p):
        arrived([q_copy(p, 0, x_prv, 0, nxt), q_copy(p, 1, x_nxt, 1, prv)])
        begin([q_copy(p, 4, x_prv, 0, nxt), q_copy(p, 5, x_nxt, 1, prv)])

    def q_done(p):
        arrived(
            [
                q_copy(p, 2, x_prv, 1, nxt),
                q_copy(p, 3, x_nxt, 0, prv),
                q_copy(p, 4, x_far, 0, nxt),
                q_copy(p, 5, x_far, 1, prv),
            ]
        )

    def project_half(p):
        for i in range(2):
            rows = pl.ds((2 * p + i) * 2 * ROWS, 2 * ROWS)
            weights = (wq0, wq1)[p][:, :, :, :, i * HD : (i + 1) * HD]
            qb[rows, :] = rotated(normed(project(weights), qg)).astype(jnp.bfloat16)

    arrived(k3)
    arrived(q02)
    q_hop1(0)
    keys = rotated(normed(project(wk[...]), kg)).astype(jnp.bfloat16)
    own = [kv.at[SLOT["a0"], 0], kv.at[SLOT["b0"], 0]]
    for i in range(2):
        own[i][:ROWS] = keys[i * ROWS : (i + 1) * ROWS]
        own[i][ROWS : ROWS + 16] = jnp.concatenate([idb[i], idb[i]], axis=-1)
    arrived(v3)
    values = normed(project(wv[...]), None).astype(jnp.bfloat16)
    for i in range(2):
        own[i][ROWS + 16 :] = values[i * ROWS : (i + 1) * ROWS]

    to_z = (along("z", 1), along("z", NZ - 1))

    def at(kind, planes, lane):
        return kv.at[SLOT[kind + str(planes % NZ)], lane]

    def planes_after(way, hops):
        return (NZ - hops) % NZ if way == 0 else hops

    def a_copy(way, hop, lane):
        src = at("a", planes_after(way, hop - 1), lane)
        dst = at("a", planes_after(way, hop), lane)
        sem = (way, hop - 1, lane)
        return remote(src, dst, s_a.at[sem], r_a.at[sem], to_z[way])

    def b_copy(way, hop):
        src = at("b", planes_after(way, hop - 1), 0)
        dst = at("b", planes_after(way, hop), 0)
        if hop == NZ // 2:
            piece = pl.ds(*PIECES[way])
            src, dst = src.at[piece], dst.at[piece]
        return remote(src, dst, s_b.at[way, hop - 1], r_b.at[way, hop - 1], to_z[way])

    def y_copy(kind, planes, k):
        row = NZ if kind == "a" else planes % NZ
        off = OFFS["y"][k]
        return remote(
            at(kind, planes, 0),
            at(kind, planes, NY - off),
            s_y.at[row, k],
            r_y.at[row, k],
            along("y", off),
        )

    def a_ways(hop, lane):
        if hop < NZ // 2:
            return (0, 1)
        return (0,) if lane < NY // 2 else (1,)

    def a_send(hop, lane):
        begin([a_copy(way, hop, lane) for way in a_ways(hop, lane)])

    def a_arrive(hop, forward):
        for lane in range(NY):
            for way in a_ways(hop, lane):
                a_copy(way, hop, lane).wait_recv()
            if forward:
                for way in a_ways(hop + 1, lane):
                    begin([a_copy(way, hop + 1, lane)])

    def y_send(kind, planes):
        begin([y_copy(kind, planes, k) for k in range(NY - 1)])

    def y_arrive(kind, planes):
        arrived([y_copy(kind, planes, k) for k in range(NY - 1)])

    def b_arrive(hop):
        for way in range(2):
            b_copy(way, hop).wait_recv()
            if hop < NZ // 2:
                begin([b_copy(way, hop + 1)])
                y_send("b", planes_after(way, hop))
        if hop == NZ // 2:
            y_send("b", hop)

    begin([b_copy(way, 1) for way in range(2)])
    y_send("a", 0)
    a_send(1, 0)
    y_send("b", 0)

    def repeat(lo, hi, f):
        def go(t, carry):
            f(t)
            return carry

        lax.fori_loop(lo, hi, go, 0)

    limit = length[0].astype(jnp.float32)
    lane = lax.broadcasted_iota(jnp.int32, (1, ROWS), 1)
    lane_in_block = (lane % (ROWS // 2)).astype(jnp.float32)

    def attend(group, pair):
        units = [kv[group, i] for i in range(NY)]
        key_pos = []
        for u in units:
            number = u[ROWS : ROWS + 16, :ROWS].astype(jnp.float32)[:1]
            key_pos.append(number * (ROWS // 2) + lane_in_block)
        seen = [jnp.where(kp < limit, kp, 1e9) for kp in key_pos]
        keys = jnp.concatenate([u[:ROWS] for u in units], axis=0)
        values = jnp.concatenate([u[ROWS + 16 :] for u in units], axis=0)

        def head(h):
            rows = pl.ds(pl.multiple_of((2 * pair + h) * 2 * ROWS, 2 * ROWS), 2 * ROWS)
            query_pos = metab[:, HD : HD + ROWS]
            scores = lax.dot_general(
                qb[rows, :], keys, (((1,), (1,)), ((), ())), preferred_element_type=jnp.float32
            )
            parts = [
                jnp.where(sn <= query_pos, scores[:, i * ROWS : (i + 1) * ROWS], FLOOR_SCORE)
                for i, sn in enumerate(seen)
            ]
            old_max = mb[rows, :]
            top = parts[0]
            for part in parts[1:]:
                top = jnp.maximum(top, part)
            new_max = jnp.maximum(old_max, jnp.max(top, axis=-1, keepdims=True))
            rescale = jnp.exp(old_max - new_max)
            weights = [jnp.exp(part - new_max) for part in parts]
            total = weights[0]
            for wt in weights[1:]:
                total = total + wt
            mb[rows, :] = new_max
            lb[rows, :] = lb[rows, :] * rescale + total
            product = jnp.dot(
                jnp.concatenate([wt.astype(jnp.bfloat16) for wt in weights], axis=-1),
                values,
                preferred_element_type=jnp.float32,
            )
            acc[rows, :] = acc[rows, :] * jnp.concatenate([rescale, rescale], axis=-1) + product

        for h in range(2):
            head(h)

        def page_part(i):
            rows = pl.ds(pl.multiple_of(i * 2 * ROWS, 2 * ROWS), 2 * ROWS)
            wanted = tpos[rows, :]
            chosen = jnp.concatenate(
                [jnp.where(wanted == kp, 1.0, 0.0).astype(jnp.bfloat16) for kp in key_pos], axis=-1
            )
            pacc[rows, :HD] += jnp.dot(chosen, keys, preferred_element_type=jnp.float32)
            pacc[rows, HD:] += jnp.dot(chosen, values, preferred_element_type=jnp.float32)

        page_part(pair)

    def attend_groups(lo, hi, pair):
        repeat(lo, hi, lambda g: attend(g, pair))

    y_arrive("a", 0)
    for lane in range(1, NY):
        a_send(1, lane)
    b_arrive(1)
    q_hop2(0)
    arrived(q12)
    q_hop1(1)
    a_arrive(1, True)
    q_done(0)
    project_half(0)
    y_arrive("b", 0)
    attend_groups(0, 4, 0)
    b_arrive(2)
    q_hop2(1)
    for planes in (1, 7):
        y_arrive("b", planes)
    attend_groups(4, 6, 0)
    a_arrive(2, True)
    attend_groups(6, 8, 0)
    b_arrive(3)
    q_done(1)
    project_half(1)
    attend_groups(0, 6, 1)
    for planes in (2, 6):
        y_arrive("b", planes)
    attend_groups(8, 10, 0)
    a_arrive(3, True)
    b_arrive(4)
    attend_groups(10, 12, 0)
    attend_groups(6, 12, 1)
    for planes in (3, 5):
        y_arrive("b", planes)
    repeat(0, 4, lambda i: attend(12 + i // 2, i % 2))
    a_arrive(4, False)
    y_arrive("b", 4)
    repeat(0, 4, lambda i: attend(14 + i // 2, i % 2))

    def result(part, h):
        start = h * 2 * ROWS + part * ROWS
        rows = pl.ds(pl.multiple_of(start, ROWS), ROWS)
        live = metab[pl.ds(pl.multiple_of(part * ROWS, ROWS), ROWS), HD : HD + 1] < limit
        total = jnp.sum(lb[rows, :], axis=-1, keepdims=True)
        divided = acc[rows, :] / jnp.where(live, total, 1.0)
        return jnp.where(live, divided, 0.0).astype(jnp.bfloat16)

    for h in range(GRP):
        osend[:, h * HD : (h + 1) * HD] = result(1 - c, h)
    o_cp = remote(osend, orecv, s_sib.at[4], r_sib.at[4], sib)
    o_cp.start()
    half = 4 * 64
    theirs = pl.ds(pl.multiple_of((1 - c) * half, half), half)
    psend[...] = pacc[theirs, :].astype(jnp.bfloat16)
    p_cp = remote(psend, precv, s_sib.at[5], r_sib.at[5], sib)
    p_cp.start()
    my_cols = pl.multiple_of(c * GRP * HD, GRP * HD)
    for h in range(GRP):
        out[:, pl.ds(my_cols + h * HD, HD)] = result(c, h)
    p_cp.wait()
    ours = pl.ds(pl.multiple_of(c * half, half), half)
    pages[...] = (pacc[ours, :] + precv[...].astype(jnp.float32)).astype(jnp.bfloat16)
    o_cp.wait()
    out[:, pl.ds(pl.multiple_of((1 - c) * GRP * HD, GRP * HD), GRP * HD)] = orecv[...]

    for cp in sends:
        cp.wait_send()


def body(tokens, block_ids, lengths, page_table, qkv_weight, q_gain, k_gain):
    half = HD // 2
    channel = jnp.arange(half).astype(jnp.float32)
    inverse = jnp.power(jnp.float32(ROPE_BASE), -2.0 * channel / HD)
    vm = pl.BlockSpec(memory_space=pltpu.VMEM)
    dma = pltpu.SemaphoreType.DMA
    bf, f32 = jnp.bfloat16, jnp.float32
    attended, cache = pl.pallas_call(
        kernel,
        out_shape=(
            jax.ShapeDtypeStruct((ROWS, H * HD), bf),
            jax.ShapeDtypeStruct((4 * 64, 2 * HD), bf),
        ),
        in_specs=[vm] * 6 + [pl.BlockSpec(memory_space=pltpu.SMEM)] * 2,
        out_specs=(vm, vm),
        scratch_shapes=[
            pltpu.VMEM((2 * ROWS, 2048), bf),
            pltpu.VMEM((2 * ROWS, 3 * ROWS), f32),
            pltpu.VMEM((2, 16, ROWS), bf),
            pltpu.VMEM((8 * 64, ROWS), f32),
            pltpu.VMEM((8, 6 * HD), bf),
            pltpu.VMEM((8, 6 * HD), bf),
            pltpu.VMEM((NX, NZ, NY, 16, HD), bf),
            pltpu.VMEM((NX, NZ, NY, 16, HD), bf),
            pltpu.VMEM((NX, NZ, NY, 16, 2 * HD), bf),
            pltpu.VMEM((NX, NZ, NY, 16, 2 * HD), bf),
            pltpu.VMEM((2 * NZ, NY, UNIT, HD), bf),
            pltpu.VMEM((GRP * 2 * ROWS, HD), bf),
            pltpu.VMEM((GRP * 2 * ROWS, ROWS), f32),
            pltpu.VMEM((GRP * 2 * ROWS, ROWS), f32),
            pltpu.VMEM((GRP * 2 * ROWS, HD), f32),
            pltpu.VMEM((8 * 64, 2 * HD), f32),
            pltpu.VMEM((ROWS, GRP * HD), bf),
            pltpu.VMEM((ROWS, GRP * HD), bf),
            pltpu.VMEM((4 * 64, 2 * HD), bf),
            pltpu.VMEM((4 * 64, 2 * HD), bf),
            dma((6,)),
            dma((6,)),
            dma((10, 7)),
            dma((10, 7)),
            dma((2, 6)),
            dma((2, 6)),
            dma((2, NZ // 2, NY)),
            dma((2, NZ // 2, NY)),
            dma((2, NZ // 2)),
            dma((2, NZ // 2)),
            dma((NZ + 1, NY - 1)),
            dma((NZ + 1, NY - 1)),
            dma((1,)),
        ],
        compiler_params=pltpu.CompilerParams(
            collective_id=0, has_side_effects=True, vmem_limit_bytes=56 << 20
        ),
        name="prefill",
    )(
        tokens[0],
        qkv_weight,
        q_gain.reshape(1, HD),
        k_gain.reshape(1, HD),
        inverse.reshape(1, half),
        page_table[0],
        block_ids[0],
        lengths,
    )
    return (attended[None], cache.reshape(1, 4, 64, 2 * HD))


def solution(mesh):
    in_specs = (
        P("req", "blk", None),
        P("req", "blk"),
        P("req"),
        P("req", None, None),
        P(("req", "blk"), None),
        P(),
        P(),
    )
    out_specs = (P("req", "blk", None), P("req", "blk", None, None))
    return jax.shard_map(body, mesh=mesh, in_specs=in_specs, out_specs=out_specs, check_vma=False)
```

time: 130 us -> 117 us (0.900)
  Pallas kernels: 121 us -> 113 us
  local copies, waits for them, and re-layouts: 5.21 us -> 2.63 us
  other arithmetic: 2 us -> 0.52 us
    pallas_call x1, Pallas kernels: 121 us -> 113 us  [body(): pl.pallas_call(kernel, out_shape=(jax.ShapeDtypeStruct((ROWS, H * HD), bf...]
    broadcast_in_dim x3 -> x0, local copies, waits for them, and re-layouts: 1.5 us -> none  [the longest x1 0.84 us: body(): jnp.broadcast_to(wanted.reshape(8 * blk_rows, 1).astype(jnp.float32), (8...]
    unnamed x10 -> x4, local copies, waits for them, and re-layouts: 3.22 us -> 2.63 us
where the time goes in v3:
time: 117 us
  Pallas kernels  113 us (97%)
  local copies, waits for them, and re-layouts  2.63 us (2%)
  between operations  1.29 us (1%)
    pallas_call x1, Pallas kernels, body(): pl.pallas_call(kernel, out_shape=(jax.ShapeDtypeStruct((ROWS, H * HD), bf...  113 us
    unnamed x4, local copies, waits for them, and re-layouts  2.63 us

profile of v3, /device:TPU:1, one launch (start us, length us, event | category | flops | bytes accessed | tf_op | source)
XLA Modules:
  0.0 117.4 jit_solution(17728381018587207692)
XLA Ops:
  1.3 0.5 multiply_power_fusion.inverse
  1.8 112.9 %prefill.1 = (bf16[128,2048]{1,0:T(8,128)(2,1)}, bf16[256,512]{1,0:T(8,128)(2,1)}) custom-call(bf16[128,2048]{1,0:T(8,128)(2,1)} %bitcast.7, bf16[8,3072]{1,0:T(8,128)(2,1)} %w.1, f32[1,256]{1,0:T(1,128)} %bitcast.10, f32[1,256]{1,0:T(1,128)} %bitcast.11, f32[1,128]{1,0:T(1,128)} %multiply_power_fusion.inverse, s32[2,128]{1,0:T(2,128)} %bitcast.12, ...), custom_call_target="tpu_custom_call" | custom-call | tf_op jit(solution)/shard_map/prefill/pallas_call | solution.py:473
  114.7 0.0 copy-start
  114.7 1.9 %copy.12 = bf16[1,128,2048]{2,1,0:T(8,128)(2,1)} copy(bf16[1,128,2048]{2,1,0:T(8,128)(2,1)} %bitcast.8) | data formatting | bytes 1048576
  116.7 0.0 copy-done
  116.7 0.7 copy.13
Async XLA Ops:
  114.7 1.9 %copy-start = (bf16[256,512]{1,0:T(8,128)(2,1)S(1)}, bf16[256,512]{1,0:T(8,128)(2,1)}, u32[]{:S(2)}) copy-start(bf16[256,512]{1,0:T(8,128)(2,1)} %get-tuple-element.5) | copy-start | bytes 786436

commit v4 on v3

--- a/solution.py
+++ b/solution.py
@@ -423,9 +423,10 @@
         y_arrive("b", planes)
     attend_groups(8, 10, 0)
     a_arrive(3, True)
+    attend_groups(10, 12, 0)
+    attend_groups(6, 9, 1)
     b_arrive(4)
-    attend_groups(10, 12, 0)
-    attend_groups(6, 12, 1)
+    attend_groups(9, 12, 1)
     for planes in (3, 5):
         y_arrive("b", planes)
     repeat(0, 4, lambda i: attend(12 + i // 2, i % 2))

time: 117 us -> 117 us (level)
  no operation moved by 1% of the time
where the time goes in v4:
time: 117 us; the launch traced here: 116 us
  Pallas kernels  112 us (96%)
  local copies, waits for them, and re-layouts  2.63 us (2%)
  between operations  1.29 us (1%)
    pallas_call x1, Pallas kernels, body(): pl.pallas_call(kernel, out_shape=(jax.ShapeDtypeStruct((ROWS, H * HD), bf...  112 us
    unnamed x4, local copies, waits for them, and re-layouts  2.63 us

profile of v4, /device:TPU:1, one launch (start us, length us, event | category | flops | bytes accessed | tf_op | source)
XLA Modules:
  0.0 116.4 jit_solution(15274651962011849134)
XLA Ops:
  1.3 0.5 multiply_power_fusion.inverse
  1.8 111.9 %prefill.1 = (bf16[128,2048]{1,0:T(8,128)(2,1)}, bf16[256,512]{1,0:T(8,128)(2,1)}) custom-call(bf16[128,2048]{1,0:T(8,128)(2,1)} %bitcast.7, bf16[8,3072]{1,0:T(8,128)(2,1)} %w.1, f32[1,256]{1,0:T(1,128)} %bitcast.10, f32[1,256]{1,0:T(1,128)} %bitcast.11, f32[1,128]{1,0:T(1,128)} %multiply_power_fusion.inverse, s32[2,128]{1,0:T(2,128)} %bitcast.12, ...), custom_call_target="tpu_custom_call" | custom-call | tf_op jit(solution)/shard_map/prefill/pallas_call | solution.py:474
  113.7 0.0 copy-start
  113.7 1.9 %copy.12 = bf16[1,128,2048]{2,1,0:T(8,128)(2,1)} copy(bf16[1,128,2048]{2,1,0:T(8,128)(2,1)} %bitcast.8) | data formatting | bytes 1048576
  115.7 0.0 copy-done
  115.7 0.7 copy.13
Async XLA Ops:
  113.7 1.9 %copy-start = (bf16[256,512]{1,0:T(8,128)(2,1)S(1)}, bf16[256,512]{1,0:T(8,128)(2,1)}, u32[]{:S(2)}) copy-start(bf16[256,512]{1,0:T(8,128)(2,1)} %get-tuple-element.5) | copy-start | bytes 786436
